TPU v7x, 32 devices: a whole 2x2x4 slice. The times are simulated.
32 devices in a mesh: kgrp: 4 (over x, core), band: 8 (over z, y).
Axes of the slice: x: 2, y: 2, z: 4, core: 2. Of those that a mesh axis runs over, the one named last changes fastest.
Arguments:
- densities: bfloat16 [8, 128, 128, 4096], P('kgrp', 'band'), may hold values from -6 to 6
- amplitudes: bfloat16 [8, 8, 128, 128], P('kgrp'), may hold values from -0.046875 to 0.046875
- partner: int32 [8], replicated, may hold values from 0 to 7, as said below
- qtable: int32 [8], replicated, may hold values from 0 to 63
- grid_map: int32 [64, 4096], replicated, may hold values from 0 to 4095, each once within a row
- coulomb: float32 [64, 4096], replicated, may hold values from 0.5 to 2
Outputs:
- ladder: bfloat16 [128, 8, 8, 128], P('band', 'kgrp')
Inputs may be any that keep to these rules, and one draw needn't show every extreme that they name: partner is a permutation of the 8 k-pairs; k-pair r lies in group r // 2. The two pairs of a group have their partners in two different groups, neither of them the group itself, and the two pairs whose partners lie in one group belong to two different groups. `grid_map`: each row is a permutation of the 4096 grid positions.
All inputs are finite; a program needn't handle non-finite values.
Results may differ from a plain program's by a relative error of at most 0.0064.
Values may be sent and summed in bfloat16 or wider, within the bound.
A program may use at most 448 MiB of HBM per device.

v0:
```python
import functools
import math

import jax
import jax.numpy as jnp
from jax import lax
from jax.experimental import pallas as pl
from jax.experimental.pallas import tpu as pltpu
from jax.sharding import PartitionSpec as P

CUTS = (3, 8, 4, 1)


def turn_kernel(source_ref, out_ref):
    rows, width, count = source_ref.shape[1:]
    flat = source_ref[0].reshape(rows * width, count)
    out_ref[0] = flat.T.reshape(count, rows, width)


def turn(densities, pair):
    _, rows, width, g_all = densities.shape
    count = math.gcd(g_all, 256)
    moved = rows * width * g_all
    return pl.pallas_call(
        turn_kernel,
        grid=(g_all // count,),
        in_specs=[pl.BlockSpec((1, rows, width, count), lambda g: (pair, 0, 0, g))],
        out_specs=pl.BlockSpec((1, count, rows, width), lambda g: (0, g, 0, 0)),
        out_shape=jax.ShapeDtypeStruct((1, g_all, rows, width), densities.dtype),
        cost_estimate=pl.CostEstimate(flops=moved, bytes_accessed=4 * moved, transcendentals=0),
        name="turn",
    )(densities)


def pick_kernel(index_ref, factor_ref, *refs):
    *source_refs, out_ref = refs
    devices, _, depth = out_ref.shape[:3]

    def one_pair(pair, source_ref):
        def one(i, carry):
            d, g = i // depth, lax.rem(i, depth)
            row = source_ref[0, index_ref[pair, i]].astype(jnp.float32) * factor_ref[pair, i]
            out_ref[d, 0, g] = row.astype(out_ref.dtype)
            return carry

        lax.fori_loop(0, devices * depth, one, 0, unroll=8)

    for pair, source_ref in enumerate(source_refs):
        pl.when(pl.program_id(0) == pair)(functools.partial(one_pair, pair, source_ref))


def pick_rows(sources, index, factors):
    pairs = len(sources)
    _, g_all, rows, width = sources[0].shape
    devices, depth = index.shape[1:]
    moved = pairs * devices * depth * rows * width
    return pl.pallas_call(
        pick_kernel,
        grid_spec=pltpu.PrefetchScalarGridSpec(
            num_scalar_prefetch=2,
            grid=(pairs,),
            in_specs=[
                pl.BlockSpec(
                    (1, g_all, rows, width), lambda p, i, f: (0, 0, 0, 0), pipeline_mode=pl.Buffered(1)
                )
            ] * pairs,
            out_specs=pl.BlockSpec((devices, 1, depth, rows, width), lambda p, i, f: (0, p, 0, 0, 0)),
        ),
        out_shape=jax.ShapeDtypeStruct((devices, pairs, depth, rows, width), sources[0].dtype),
        cost_estimate=pl.CostEstimate(
            flops=moved, bytes_accessed=2 * pairs * sources[0].size + 2 * moved, transcendentals=0
        ),
        compiler_params=pltpu.CompilerParams(vmem_limit_bytes=62 * 1024 * 1024),
        name="pick_rows",
    )(index.reshape(pairs, -1), factors.reshape(pairs, -1), *sources)


def ladder_kernel(partner_ref, slot_ref, left_ref, right_ref, amp_ref, *rest):
    out_ref, total = rest[-2], rest[-1]
    step, last = pl.program_id(1), pl.num_programs(1) - 1
    bands, _, depth, rows, width = left_ref.shape[1:]
    vb = bands * rows
    slabs = amp_ref.shape[2] // width
    left = jnp.concatenate([left_ref[0, :, 0, g].reshape(vb, width) for g in range(depth)], axis=0)
    right = jnp.concatenate([right_ref[0, :, 0, g].reshape(vb, width) for g in range(depth)], axis=1)
    mixed = jnp.dot(left, amp_ref[0], preferred_element_type=jnp.float32).astype(jnp.bfloat16)
    wide = jnp.concatenate(
        [
            jnp.concatenate(
                [mixed[g * vb:(g + 1) * vb, s * width:(s + 1) * width] for g in range(depth)], axis=1
            )
            for s in range(slabs)
        ],
        axis=0,
    )
    part = lax.dot_general(wide, right, (((1,), (1,)), ((), ())), preferred_element_type=jnp.float32)

    @pl.when(step == 0)
    def _():
        total[...] = part if len(rest) == 2 else part + rest[0][0]

    @pl.when(step > 0)
    def _():
        total[...] += part

    @pl.when(step == last)
    def _():
        out_ref[0] = total[...].astype(out_ref.dtype)


def ladder_sums(blocks, amps, partner, slots, before, kind):
    groups, bands, per_group, g_count, rows, width = blocks.shape
    pairs = per_group * groups
    vb = bands * rows
    depth = math.gcd(g_count, 8)
    slabs = amps.shape[2] // width

    def left_map(r, s, partner_ref, slot_ref):
        return (r // per_group, 0, lax.rem(r, per_group), s, 0, 0)

    def right_map(r, s, partner_ref, slot_ref):
        q = partner_ref[r]
        return (q // per_group, 0, lax.rem(q, per_group), s, 0, 0)

    def amp_map(r, s, partner_ref, slot_ref):
        return (slot_ref[r // per_group] * per_group + lax.rem(r, per_group), 0, 0)

    spec = (1, bands, 1, depth, rows, width)
    sum_spec = pl.BlockSpec((1, slabs * vb, vb), lambda r, s, p, q: (r, 0, 0))
    return pl.pallas_call(
        ladder_kernel,
        grid_spec=pltpu.PrefetchScalarGridSpec(
            num_scalar_prefetch=2,
            grid=(pairs, g_count // depth),
            in_specs=[
                pl.BlockSpec(spec, left_map),
                pl.BlockSpec(spec, right_map),
                pl.BlockSpec((1,) + amps.shape[1:], amp_map),
            ] + [sum_spec] * len(before),
            out_specs=sum_spec,
            scratch_shapes=[pltpu.VMEM((slabs * vb, vb), jnp.float32)],
        ),
        out_shape=jax.ShapeDtypeStruct((pairs, slabs * vb, vb), kind),
        cost_estimate=pl.CostEstimate(
            flops=4 * pairs * g_count * vb * vb * vb * slabs, bytes_accessed=4 * blocks.size, transcendentals=0
        ),
        name="ladder",
    )(partner, slots, blocks, blocks, amps, *before)


def shards(group_count, band_count, densities, amplitudes, partner, qtable, grid_map, coulomb):
    my_group = lax.axis_index("kgrp")
    per_group, rows, width, g_all = densities.shape
    slabs = amplitudes.shape[1]
    vb = rows * band_count
    devices = group_count * band_count
    g_shard = g_all // devices
    own_ids = my_group * per_group + jnp.arange(per_group, dtype=jnp.int32)
    transfers = jnp.take(qtable, own_ids)
    positions = jnp.take(grid_map, transfers, axis=0).reshape(per_group, devices, g_shard)
    factors = jnp.take(coulomb, transfers, axis=0).reshape(per_group, devices, g_shard)
    held = jnp.transpose(amplitudes, (0, 2, 1, 3)).reshape(per_group, width, slabs * width)
    arrived = [held]
    for shift in range(1, group_count):
        ring = [(source, (source + shift) % group_count) for source in range(group_count)]
        arrived.append(lax.ppermute(held, "kgrp", ring))
    amps = jnp.concatenate(arrived, axis=0)
    slots = lax.rem(my_group - jnp.arange(group_count, dtype=jnp.int32) + group_count, group_count)

    unit = sum(CUTS)
    counts = [g_shard * cut // unit for cut in CUTS] if g_shard % unit == 0 else [g_shard]
    starts = [sum(counts[:at]) for at in range(len(counts))]

    def exchange(chunk):
        return lax.all_to_all(chunk, ("kgrp", "band"), split_axis=0, concat_axis=0, tiled=True)

    def pick(at, first, count):
        span = slice(starts[at], starts[at] + counts[at])
        own = slice(first, first + count)
        return pick_rows(turned[own], positions[own, :, span], factors[own, :, span])

    turned, firsts, source = [], [], densities
    for p in range(per_group):
        turned.append(turn(source, p))
        chunk = pick(0, p, 1)
        chunk, source = lax.optimization_barrier((chunk, source))
        firsts.append(exchange(chunk))
    tables = [jnp.concatenate(firsts, axis=1)]

    before = ()

    def add_sums(at):
        kind = jnp.bfloat16 if at == len(counts) - 1 else jnp.float32
        blocks = tables[at].reshape(group_count, band_count, per_group, counts[at], rows, width)
        return (ladder_sums(blocks, amps, partner, slots, before, kind),)

    for at in range(1, len(counts)):
        chunk = pick(at, 0, per_group)
        if at > 1:
            before = add_sums(at - 2)
            chunk, *before = lax.optimization_barrier((chunk, *before))
        tables.append(exchange(chunk))
    for at in range(max(len(counts) - 2, 0), len(counts)):
        before = add_sums(at)

    sums = before[0].reshape(group_count, per_group, slabs, band_count, rows, vb)
    sums = jnp.transpose(sums, (0, 3, 1, 2, 4, 5)).reshape(devices, per_group, slabs, rows, vb)
    sums = lax.all_to_all(sums, ("kgrp", "band"), split_axis=0, concat_axis=0, tiled=True)
    summed = jnp.sum(sums.astype(jnp.float32), axis=0) * (1.0 / math.sqrt(g_all))
    return jnp.transpose(summed, (2, 0, 1, 3)).astype(jnp.bfloat16)


def solution(mesh):
    in_specs = (P("kgrp", "band", None, None), P("kgrp", None, None, None), P(), P(), P(), P())
    out_specs = P("band", "kgrp", None, None)
    body = functools.partial(shards, mesh.shape["kgrp"], mesh.shape["band"])
    return jax.shard_map(body, mesh=mesh, in_specs=in_specs, out_specs=out_specs, check_vma=False)
```

profile of v0, /device:TPU:0, one launch (start us, length us, event | category | flops | bytes accessed | tf_op | source)
XLA Modules:
  0.0 902.5 jit_solution(11984950354443412854)
XLA Ops:
  0.0 1.4 gather_fusion
  1.5 0.6 gather_fusion.2
  2.0 1.8 gather_fusion.1
  4.0 0.7 reshape.118.index_ref
  4.7 0.7 reshape.119.factor_ref
  5.4 20.2 %turn.2.refs_0_ = bf16[1,4096,16,128]{3,2,1,0:T(8,128)(2,1)} custom-call(bf16[2,16,128,4096]{3,2,1,0:T(8,128)(2,1)} %source_ref.2), custom_call_target="tpu_custom_call" | custom-call | flops 8388608 | bytes 33554432 | tf_op jit(solution)/shard_map/turn/pallas_call | solution.py:24
  25.5 14.3 %pick_rows.5 = bf16[32,1,24,16,128]{4,3,2,1,0:T(8,128)(2,1)} custom-call(s32[1,768]{1,0:T(1,128)} %reshape.118.index_ref, f32[1,768]{1,0:T(1,128)} %reshape.119.factor_ref, bf16[1,4096,16,128]{3,2,1,0:T(8,128)(2,1)} %turn.2.refs_0_), custom_call_target="tpu_custom_call" | custom-call | flops 1572864 | bytes 19922944 | tf_op jit(solution)/shard_map/pick_rows/pallas_call | solution.py:57
  39.8 7.4 all-to-all-start.1
  47.3 0.7 reshape.126.index_ref
  48.0 0.7 reshape.127.factor_ref
  48.6 20.2 %turn.3.refs_1_.refs_0_ = bf16[1,4096,16,128]{3,2,1,0:T(8,128)(2,1)} custom-call(bf16[2,16,128,4096]{3,2,1,0:T(8,128)(2,1)} %source_ref.2), custom_call_target="tpu_custom_call" | custom-call | flops 8388608 | bytes 33554432 | tf_op jit(solution)/shard_map/turn/pallas_call | solution.py:24
  68.8 14.3 %pick_rows.9 = bf16[32,1,24,16,128]{4,3,2,1,0:T(8,128)(2,1)} custom-call(s32[1,768]{1,0:T(1,128)} %reshape.126.index_ref, f32[1,768]{1,0:T(1,128)} %reshape.127.factor_ref, bf16[1,4096,16,128]{3,2,1,0:T(8,128)(2,1)} %turn.3.refs_1_.refs_0_), custom_call_target="tpu_custom_call" | custom-call | flops 1572864 | bytes 19922944 | tf_op jit(solution)/shard_map/pick_rows/pallas_call | solution.py:57
  83.1 37.1 %all-to-all-done.1 = bf16[32,1,24,16,128]{4,3,2,1,0:T(8,128)(2,1)} async-done(((bf16[32,1,24,16,128]{4,3,2,1,0:T(8,128)(2,1)}), bf16[32,1,24,16,128]{4,3,2,1,0:T(8,128)(2,1)}, u32[]{:S(2)}, u32[]{:S(2)}) %all-to-all-start.1) | async-done | bytes 3145760 | tf_op jit(solution)/shard_map/all_to_all | solution.py:175
  120.2 3.6 all-to-all-start.2
  123.9 0.7 reshape.120.index_ref
  124.6 0.7 reshape.121.factor_ref
  125.3 50.9 %pick_rows.7 = bf16[32,2,64,16,128]{4,3,2,1,0:T(8,128)(2,1)} custom-call(s32[2,2048]{1,0:T(2,128)} %reshape.120.index_ref, f32[2,2048]{1,0:T(2,128)} %reshape.121.factor_ref, bf16[1,4096,16,128]{3,2,1,0:T(8,128)(2,1)} %turn.2.refs_0_, bf16[1,4096,16,128]{3,2,1,0:T(8,128)(2,1)} %turn.3.refs_1_.refs_0_), custom_call_target="tpu_custom_call" | custom-call | flops 8388608 | bytes 50331648 | tf_op jit(solution)/shard_map/pick_rows/pallas_call | solution.py:57
  176.2 20.6 %all-to-all-done.2 = bf16[32,1,24,16,128]{4,3,2,1,0:T(8,128)(2,1)} async-done(((bf16[32,1,24,16,128]{4,3,2,1,0:T(8,128)(2,1)}), bf16[32,1,24,16,128]{4,3,2,1,0:T(8,128)(2,1)}, u32[]{:S(2)}, u32[]{:S(2)}) %all-to-all-start.2) | async-done | bytes 3145760 | tf_op jit(solution)/shard_map/all_to_all | solution.py:175
  196.8 3.9 all-to-all-start
  200.8 1.6 collective-permute-start.1
  202.5 1.3 collective-permute-start.2
  203.8 0.6 compare_select_fusion.4.slot_ref
  204.6 0.7 reshape.124.index_ref
  205.3 0.7 reshape.125.factor_ref
  205.9 31.4 %pick_rows.8 = bf16[32,2,32,16,128]{4,3,2,1,0:T(8,128)(2,1)} custom-call(s32[2,1024]{1,0:T(2,128)} %reshape.124.index_ref, f32[2,1024]{1,0:T(2,128)} %reshape.125.factor_ref, bf16[1,4096,16,128]{3,2,1,0:T(8,128)(2,1)} %turn.2.refs_0_, bf16[1,4096,16,128]{3,2,1,0:T(8,128)(2,1)} %turn.3.refs_1_.refs_0_), custom_call_target="tpu_custom_call" | custom-call | flops 4194304 | bytes 41943040 | tf_op jit(solution)/shard_map/pick_rows/pallas_call | solution.py:57
  237.4 0.9 constant_dynamic-update-slice_fusion.3
  238.3 81.2 %collective-permute-done = bf16[2,128,1024]{2,1,0:T(8,128)(2,1)} collective-permute-done((bf16[2,128,1024]{2,1,0:T(8,128)(2,1)S(1)}, bf16[2,128,1024]{2,1,0:T(8,128)(2,1)}, u32[]{:S(2)}, u32[]{:S(2)}) %collective-permute-start) | collective-permute-done | bytes 524320 | tf_op jit(solution)/shard_map/ppermute | solution.py:166
  319.5 1.9 constant_dynamic-update-slice_fusion.2
  321.4 8.4 collective-permute-done.1
  329.7 1.9 constant_dynamic-update-slice_fusion.1
  331.6 17.5 %collective-permute-done.2 = bf16[2,128,1024]{2,1,0:T(8,128)(2,1)} collective-permute-done((bf16[2,128,1024]{2,1,0:T(8,128)(2,1)S(1)}, bf16[2,128,1024]{2,1,0:T(8,128)(2,1)}, u32[]{:S(2)}, u32[]{:S(2)}) %collective-permute-start.2) | collective-permute-done | bytes 524320 | tf_op jit(solution)/shard_map/ppermute | solution.py:166
  349.2 1.9 constant_dynamic-update-slice_fusion.amp_ref
  351.1 6.2 pad_maximum_fusion
  357.3 43.2 %ladder.4.rest_0_ = f32[8,1024,128]{2,1,0:T(8,128)} custom-call(s32[8]{0:T(128)} %partner_ref.7, s32[4]{0:T(128)} %compare_select_fusion.4.slot_ref, bf16[4,8,2,24,16,128]{5,4,3,2,1,0:T(8,128)(2,1)} %bitcast.35, bf16[4,8,2,24,16,128]{5,4,3,2,1,0:T(8,128)(2,1)} %bitcast.36, bf16[8,128,1024]{2,1,0:T(8,128)(2,1)} %constant_dynamic-update-slice_fusion.amp_ref), custom_call_target="tpu_custom_call" | custom-call | flops 12884901888 | bytes 12582912 | tf_op jit(solution)/shard_map/ladder/pallas_call | solution.py:130
  400.5 175.2 %all-to-all-done = bf16[32,2,64,16,128]{4,3,2,1,0:T(8,128)(2,1)} async-done(((bf16[32,2,64,16,128]{4,3,2,1,0:T(8,128)(2,1)}), bf16[32,2,64,16,128]{4,3,2,1,0:T(8,128)(2,1)}, u32[]{:S(2)}, u32[]{:S(2)}) %all-to-all-start) | async-done | bytes 16777248 | tf_op jit(solution)/shard_map/all_to_all | solution.py:175
  575.7 3.7 all-to-all-start.4
  579.5 0.7 reshape.116.index_ref
  580.2 0.7 reshape.117.factor_ref
  580.9 16.8 %pick_rows.6 = bf16[32,2,8,16,128]{4,3,2,1,0:T(8,128)(2,1)} custom-call(s32[2,256]{1,0:T(2,128)} %reshape.116.index_ref, f32[2,256]{1,0:T(2,128)} %reshape.117.factor_ref, bf16[1,4096,16,128]{3,2,1,0:T(8,128)(2,1)} %turn.2.refs_0_, bf16[1,4096,16,128]{3,2,1,0:T(8,128)(2,1)} %turn.3.refs_1_.refs_0_), custom_call_target="tpu_custom_call" | custom-call | flops 1048576 | bytes 35651584 | tf_op jit(solution)/shard_map/pick_rows/pallas_call | solution.py:57
  597.7 111.7 %ladder.5.rest_0_ = f32[8,1024,128]{2,1,0:T(8,128)} custom-call(s32[8]{0:T(128)} %partner_ref.7, s32[4]{0:T(128)} %compare_select_fusion.4.slot_ref, bf16[4,8,2,64,16,128]{5,4,3,2,1,0:T(8,128)(2,1)} %bitcast.3.left_ref.right_ref, bf16[4,8,2,64,16,128]{5,4,3,2,1,0:T(8,128)(2,1)} %bitcast.3.left_ref.right_ref, ...), custom_call_target="tpu_custom_call" | custom-call | flops 34359738368 | bytes 33554432 | tf_op jit(solution)/shard_map/ladder/pallas_call | solution.py:130
  709.4 59.6 %all-to-all-done.4 = bf16[32,2,32,16,128]{4,3,2,1,0:T(8,128)(2,1)} async-done(((bf16[32,2,32,16,128]{4,3,2,1,0:T(8,128)(2,1)}), bf16[32,2,32,16,128]{4,3,2,1,0:T(8,128)(2,1)}, u32[]{:S(2)}, u32[]{:S(2)}) %all-to-all-start.4) | async-done | bytes 8388640 | tf_op jit(solution)/shard_map/all_to_all | solution.py:175
  769.0 2.7 all-to-all-start.3
  771.7 57.3 %ladder.6.rest_0_ = f32[8,1024,128]{2,1,0:T(8,128)} custom-call(s32[8]{0:T(128)} %partner_ref.7, s32[4]{0:T(128)} %compare_select_fusion.4.slot_ref, bf16[4,8,2,32,16,128]{5,4,3,2,1,0:T(8,128)(2,1)} %bitcast.7.left_ref.right_ref, bf16[4,8,2,32,16,128]{5,4,3,2,1,0:T(8,128)(2,1)} %bitcast.7.left_ref.right_ref, ...), custom_call_target="tpu_custom_call" | custom-call | flops 17179869184 | bytes 16777216 | tf_op jit(solution)/shard_map/ladder/pallas_call | solution.py:130
  829.0 1.4 copy-done.2
  830.4 13.3 %ladder.7 = bf16[8,1024,128]{2,1,0:T(8,128)(2,1)} custom-call(s32[8]{0:T(128)} %partner_ref.7, s32[4]{0:T(128)} %compare_select_fusion.4.slot_ref, bf16[4,8,2,8,16,128]{5,4,3,2,1,0:T(8,128)(2,1)} %bitcast.37, bf16[4,8,2,8,16,128]{5,4,3,2,1,0:T(8,128)(2,1)} %bitcast.38, bf16[8,128,1024]{2,1,0:T(8,128)(2,1)} %constant_dynamic-update-slice_fusion.amp_ref, ...), custom_call_target="tpu_custom_call" | custom-call | flops 4294967296 | bytes 4194304 | tf_op jit(solution)/shard_map/ladder/pallas_call | solution.py:130
  843.7 2.2 copy.11
  845.9 55.6 %all_to_all.30 = bf16[32,2,8,16,128]{4,3,2,1,0:T(8,128)(2,1)S(1)} all-to-all(bf16[32,2,8,16,128]{4,3,2,1,0:T(8,128)(2,1)S(1)} %bitcast.34), channel_id=1, replica_groups=mesh['kgrp'=4,'band'=8] {'kgrp','band'}, dimensions={0} | all-to-all | bytes 4194304 | tf_op jit(solution)/shard_map/all_to_all | solution.py:208
  901.8 0.6 copy.12
  (27 shorter events, 1.2 us)
Async XLA Ops:
  0.0 1.4 copy-start
  39.8 80.4 %all-to-all-start.1 = ((bf16[32,1,24,16,128]{4,3,2,1,0:T(8,128)(2,1)}), bf16[32,1,24,16,128]{4,3,2,1,0:T(8,128)(2,1)}, u32[]{:S(2)}, u32[]{:S(2)}) async-start(bf16[32,1,24,16,128]{4,3,2,1,0:T(8,128)(2,1)} %pick_rows.5), calls=%async_computation.1 | async-start | bytes 6291456 | tf_op jit(solution)/shard_map/all_to_all | solution.py:175
  120.2 76.6 %all-to-all-start.2 = ((bf16[32,1,24,16,128]{4,3,2,1,0:T(8,128)(2,1)}), bf16[32,1,24,16,128]{4,3,2,1,0:T(8,128)(2,1)}, u32[]{:S(2)}, u32[]{:S(2)}) async-start(bf16[32,1,24,16,128]{4,3,2,1,0:T(8,128)(2,1)} %pick_rows.9), calls=%async_computation.2 | async-start | bytes 6291456 | tf_op jit(solution)/shard_map/all_to_all | solution.py:175
  176.2 24.5 %copy-start.3 = (bf16[2,8,128,128]{3,2,1,0:T(8,128)(2,1)S(1)}, bf16[2,8,128,128]{3,2,1,0:T(8,128)(2,1)}, u32[]{:S(2)}) copy-start(bf16[2,8,128,128]{3,2,1,0:T(8,128)(2,1)} %param.7) | copy-start | bytes 1572868
  196.8 378.9 %all-to-all-start = ((bf16[32,2,64,16,128]{4,3,2,1,0:T(8,128)(2,1)}), bf16[32,2,64,16,128]{4,3,2,1,0:T(8,128)(2,1)}, u32[]{:S(2)}, u32[]{:S(2)}) async-start(bf16[32,2,64,16,128]{4,3,2,1,0:T(8,128)(2,1)} %pick_rows.7), calls=%async_computation | async-start | bytes 33554432 | tf_op jit(solution)/shard_map/all_to_all | solution.py:175
  200.8 118.7 %collective-permute-start = (bf16[2,128,1024]{2,1,0:T(8,128)(2,1)S(1)}, bf16[2,128,1024]{2,1,0:T(8,128)(2,1)}, u32[]{:S(2)}, u32[]{:S(2)}) collective-permute-start(bf16[2,128,1024]{2,1,0:T(8,128)(2,1)S(1)} %copy_bitcast_fusion), channel_id=1, source_target_pairs={{0,8},{8,16},{16,24},{24,0},{1,9},{9,17},{17,25},{25,1},{2,10},{10... | collective-permute-start | bytes 1572872 | tf_op jit(solution)/shard_map/ppermute | solution.py:166
  200.8 128.9 %collective-permute-start.1 = (bf16[2,128,1024]{2,1,0:T(8,128)(2,1)S(1)}, bf16[2,128,1024]{2,1,0:T(8,128)(2,1)}, u32[]{:S(2)}, u32[]{:S(2)}) collective-permute-start(bf16[2,128,1024]{2,1,0:T(8,128)(2,1)S(1)} %copy_bitcast_fusion), channel_id=1, source_target_pairs={{0,16},{8,24},{16,0},{24,8},{1,17},{9,25},{17,1},{25,9},{2,18},{10... | collective-permute-start | bytes 1572872 | tf_op jit(solution)/shard_map/ppermute | solution.py:166
  202.5 146.7 %collective-permute-start.2 = (bf16[2,128,1024]{2,1,0:T(8,128)(2,1)S(1)}, bf16[2,128,1024]{2,1,0:T(8,128)(2,1)}, u32[]{:S(2)}, u32[]{:S(2)}) collective-permute-start(bf16[2,128,1024]{2,1,0:T(8,128)(2,1)S(1)} %copy_bitcast_fusion), channel_id=1, source_target_pairs={{0,24},{8,0},{16,8},{24,16},{1,25},{9,1},{17,9},{25,17},{2,26},{10... | collective-permute-start | bytes 1572872 | tf_op jit(solution)/shard_map/ppermute | solution.py:166
  575.7 193.3 %all-to-all-start.4 = ((bf16[32,2,32,16,128]{4,3,2,1,0:T(8,128)(2,1)}), bf16[32,2,32,16,128]{4,3,2,1,0:T(8,128)(2,1)}, u32[]{:S(2)}, u32[]{:S(2)}) async-start(bf16[32,2,32,16,128]{4,3,2,1,0:T(8,128)(2,1)} %pick_rows.8), calls=%async_computation.4 | async-start | bytes 16777216 | tf_op jit(solution)/shard_map/all_to_all | solution.py:175
  769.0 60.0 %all-to-all-start.3 = ((bf16[32,2,8,16,128]{4,3,2,1,0:T(8,128)(2,1)}), bf16[32,2,8,16,128]{4,3,2,1,0:T(8,128)(2,1)S(1)}, u32[]{:S(2)}, u32[]{:S(2)}) async-start(bf16[32,2,8,16,128]{4,3,2,1,0:T(8,128)(2,1)} %pick_rows.6), calls=%async_computation.3 | async-start | bytes 4194304 | tf_op jit(solution)/shard_map/all_to_all | solution.py:175
  829.0 1.4 copy-start.2
  845.9 56.6 %copy-start.1 = (f32[64,4096]{1,0:T(8,128)S(1)}, f32[64,4096]{1,0:T(8,128)}, u32[]{:S(2)}) copy-start(f32[64,4096]{1,0:T(8,128)} %param.11) | copy-start | bytes 3145732
where the time goes:
time: 904 us; the launch traced here: 902 us
  waiting for transfers between devices  400 us (44%)
  Pallas kernels  394 us (44%)
  blocking collectives  55.6 us (6%)
  starting transfers between devices  24.4 us (3%)
  local copies, waits for them, and re-layouts  21.8 us (2%)
    all_to_all x5, waiting for transfers between devices, exchange(): lax.all_to_all(chunk, ('kgrp', 'band'), split_axis=0, concat_axis=0, tile...  292 us
    pallas_call x4, Pallas kernels, ladder_sums(): pl.pallas_call(ladder_kernel, grid_spec=pltpu.PrefetchScalarGridSpec(num_...  226 us
    pallas_call x5, Pallas kernels, pick_rows(): pl.pallas_call(pick_kernel, grid_spec=pltpu.PrefetchScalarGridSpec(num_sc...  128 us
    ppermute x3, waiting for transfers between devices, shards(): arrived.append(lax.ppermute(held, 'kgrp', ring))  107 us
    all_to_all x1, blocking collectives, shards(): lax.all_to_all(sums, ('kgrp', 'band'), split_axis=0, concat_axis=0, tiled...  55.6 us
    pallas_call x2, Pallas kernels, turn(): pl.pallas_call(turn_kernel, grid=(g_all // count,), in_specs=[pl.BlockSpe...  40.3 us
    all_to_all x5, starting transfers between devices, exchange(): lax.all_to_all(chunk, ('kgrp', 'band'), split_axis=0, concat_axis=0, tile...  21.3 us
  transfers between devices with their start and end apart: 8, of which 7 were waited for; matrix products, arithmetic and copies ran while one was open for 2% of the time, Pallas kernels for 38%

commit v1 on v0

v1 whole, which is shorter than its diff:
```python
import functools
import math

import jax
import jax.numpy as jnp
from jax import lax
from jax.experimental import pallas as pl
from jax.experimental.pallas import tpu as pltpu
from jax.sharding import PartitionSpec as P

MESH = pl.DeviceIdType.MESH
SLOTS = 3
DEPTH = 4


def fused_kernel(
    kgrp, band, partner_ref, index_ref, factor_ref, densities_ref, amplitudes_ref,
    recv_ref, out_ref,
    turned, staged, slots, block, amps, total,
    turn_sem, send_sem, recv_sem, amp_send, amp_recv, load_sem,
):
    devices = kgrp * band
    per_group, rows, width, g_all = densities_ref.shape
    rows_by_g = turned.reshape(per_group * g_all, rows, width)
    chunks = recv_ref.shape[0]
    depth = slots.shape[3]
    slabs = amps.shape[1]
    g_shard = chunks * depth
    pairs = kgrp * per_group
    vb = band * rows
    my_k, my_b = lax.axis_index("kgrp"), lax.axis_index("band")
    me = my_k * band + my_b

    def peer(m):
        return lax.rem(my_k + lax.rem(m, kgrp), kgrp), lax.rem(my_b + m // kgrp, band)

    barrier = pltpu.get_barrier_semaphore()

    def greet(m, carry):
        pl.semaphore_signal(barrier, inc=1, device_id=peer(m), device_id_type=MESH)
        return carry

    lax.fori_loop(1, devices, greet, 0)
    pl.semaphore_wait(barrier, devices - 1)

    span = staged.shape[-1]
    steps = g_all // span

    def fetch(p, i):
        return pltpu.make_async_copy(
            densities_ref.at[p, :, :, pl.ds(pl.multiple_of(i * span, span), span)],
            staged.at[lax.rem(i, 2)],
            turn_sem.at[lax.rem(i, 2)],
        )

    def turn(p):
        fetch(p, 0).start()

        def one(i, carry):
            @pl.when(i + 1 < steps)
            def _():
                fetch(p, i + 1).start()

            fetch(p, i).wait()
            flat = staged[lax.rem(i, 2)].reshape(rows * width, span)
            turned[p * steps + i] = flat.T.reshape(span, rows, width)
            return carry

        lax.fori_loop(0, steps, one, 0)

    def pick(p, chunk):
        slot = lax.rem(chunk, SLOTS)

        def one(d, carry):
            first = d * g_shard + chunk * depth
            for j in range(depth):
                row = rows_by_g[p * g_all + index_ref[p, first + j]].astype(jnp.float32) * factor_ref[p, first + j]
                slots[slot, d, p, j] = row.astype(slots.dtype)
            return carry

        lax.fori_loop(0, devices, one, 0, unroll=2)

    def send(chunk, piece):
        slot = lax.rem(chunk, SLOTS)

        def one(m, carry):
            to_k, to_b = peer(m)
            pltpu.make_async_remote_copy(
                src_ref=piece(slots.at[slot, to_k * band + to_b]),
                dst_ref=piece(recv_ref.at[chunk, me]),
                send_sem=send_sem.at[slot],
                recv_sem=recv_sem.at[chunk],
                device_id=(to_k, to_b),
                device_id_type=MESH,
            ).start()
            return carry

        lax.fori_loop(1, devices, one, 0)
        pltpu.make_async_copy(piece(slots.at[slot, me]), piece(recv_ref.at[chunk, me]), send_sem.at[slot]).start()

    def ladder(chunk):
        others = pl.ds(0, devices - 1)
        pltpu.make_async_copy(
            recv_ref.at[chunk, others], recv_ref.at[chunk, others], recv_sem.at[chunk]
        ).wait()
        load = pltpu.make_async_copy(recv_ref.at[chunk], block, load_sem)
        load.start()
        load.wait()

        def one(r, carry):
            q = partner_ref[r]
            left_base, left_pair = r // per_group * band, lax.rem(r, per_group)
            right_base, right_pair = q // per_group * band, lax.rem(q, per_group)
            left = jnp.concatenate(
                [block[left_base + b, left_pair, j] for j in range(depth) for b in range(band)], axis=0
            )
            right = jnp.concatenate(
                [
                    jnp.concatenate([block[right_base + b, right_pair, j] for b in range(band)], axis=0)
                    for j in range(depth)
                ],
                axis=1,
            )
            amp = jnp.concatenate([amps[r, s] for s in range(slabs)], axis=1)
            mixed = jnp.dot(left, amp, preferred_element_type=jnp.float32).astype(jnp.bfloat16)
            wide = jnp.concatenate(
                [
                    jnp.concatenate(
                        [mixed[j * vb:(j + 1) * vb, s * width:(s + 1) * width] for j in range(depth)], axis=1
                    )
                    for s in range(slabs)
                ],
                axis=0,
            )
            total[r] += lax.dot_general(wide, right, (((1,), (1,)), ((), ())), preferred_element_type=jnp.float32)
            return carry

        lax.fori_loop(0, pairs, one, 0)

    def amp_copy(m):
        to_k = lax.rem(my_k + m, kgrp)
        return pltpu.make_async_remote_copy(
            src_ref=amplitudes_ref,
            dst_ref=amps.at[pl.ds(my_k * per_group, per_group)],
            send_sem=amp_send,
            recv_sem=amp_recv,
            device_id=(to_k, my_b),
            device_id_type=MESH,
        )

    own_amp = pltpu.make_async_copy(amplitudes_ref, amps.at[pl.ds(my_k * per_group, per_group)], load_sem)

    def begin(p, carry):
        turn(p)
        for chunk in range(SLOTS):
            pick(p, chunk)
            if chunk:
                send(chunk - 1, lambda ref: ref.at[p])
        send(SLOTS - 1, lambda ref: ref.at[p])
        return carry

    total[...] = jnp.zeros_like(total)
    lax.fori_loop(0, per_group, begin, 0)
    own_amp.start()
    for m in range(1, kgrp):
        amp_copy(m).start()
    own_amp.wait()
    all_amps = amps.at[pl.ds(0, (kgrp - 1) * per_group)]
    pltpu.make_async_copy(all_amps, all_amps, amp_send).wait()
    pltpu.make_async_copy(all_amps, all_amps, amp_recv).wait()

    def main(chunk, carry):
        slot = lax.rem(chunk, SLOTS)
        pltpu.make_async_copy(slots.at[slot], slots.at[slot], send_sem.at[slot]).wait()

        @pl.when(chunk < chunks)
        def _():
            for p in range(per_group):
                pick(p, chunk)

        ladder(chunk - SLOTS)

        @pl.when(chunk < chunks)
        def _():
            send(chunk, lambda ref: ref)

        return carry

    lax.fori_loop(SLOTS, chunks + SLOTS, main, 0)
    out_ref[...] = total[...].astype(out_ref.dtype)


def fused(kgrp, band, densities, amplitudes, partner, index, factors):
    per_group, rows, width, g_all = densities.shape
    slabs = amplitudes.shape[1]
    devices = kgrp * band
    pairs = kgrp * per_group
    vb = rows * band
    g_shard = g_all // devices
    depth = math.gcd(g_shard, DEPTH)
    chunks = g_shard // depth
    span = math.gcd(g_all, 256)
    kind = densities.dtype
    anywhere = pl.BlockSpec(memory_space=pl.ANY)
    scalars = pl.BlockSpec(memory_space=pltpu.SMEM)
    piece = (per_group, depth, rows, width)
    return pl.pallas_call(
        functools.partial(fused_kernel, kgrp, band),
        in_specs=[scalars, scalars, scalars, anywhere, anywhere],
        out_specs=[anywhere, pl.BlockSpec(memory_space=pltpu.VMEM)],
        out_shape=[
            jax.ShapeDtypeStruct((chunks, devices) + piece, kind),
            jax.ShapeDtypeStruct((pairs, slabs * vb, vb), kind),
        ],
        scratch_shapes=[
            pltpu.VMEM((per_group * g_all // span, span, rows, width), kind),
            pltpu.VMEM((2, rows, width, span), kind),
            pltpu.VMEM((SLOTS, devices) + piece, kind),
            pltpu.VMEM((devices,) + piece, kind),
            pltpu.VMEM((pairs,) + amplitudes.shape[1:], kind),
            pltpu.VMEM((pairs, slabs * vb, vb), jnp.float32),
            pltpu.SemaphoreType.DMA((2,)),
            pltpu.SemaphoreType.DMA((SLOTS,)),
            pltpu.SemaphoreType.DMA((chunks,)),
            pltpu.SemaphoreType.DMA,
            pltpu.SemaphoreType.DMA,
            pltpu.SemaphoreType.DMA,
        ],
        compiler_params=pltpu.CompilerParams(
            collective_id=0, has_side_effects=True, vmem_limit_bytes=62 * 1024 * 1024
        ),
        name="fused",
    )(partner, index, factors, densities, amplitudes)


def shards(kgrp, band, densities, amplitudes, partner, qtable, grid_map, coulomb):
    per_group, rows, width, g_all = densities.shape
    slabs = amplitudes.shape[1]
    vb = rows * band
    devices = kgrp * band
    own_ids = lax.axis_index("kgrp") * per_group + jnp.arange(per_group, dtype=jnp.int32)
    transfers = jnp.take(qtable, own_ids)
    index = jnp.take(grid_map, transfers, axis=0)
    factors = jnp.take(coulomb, transfers, axis=0)
    _, sums = fused(kgrp, band, densities, amplitudes, partner, index, factors)
    sums = sums.reshape(kgrp, per_group, slabs, band, rows, vb)
    sums = jnp.transpose(sums, (0, 3, 1, 2, 4, 5)).reshape(devices, per_group, slabs, rows, vb)
    sums = lax.all_to_all(sums, ("kgrp", "band"), split_axis=0, concat_axis=0, tiled=True)
    summed = jnp.sum(sums.astype(jnp.float32), axis=0) * (1.0 / math.sqrt(g_all))
    return jnp.transpose(summed, (2, 0, 1, 3)).astype(jnp.bfloat16)


def solution(mesh):
    in_specs = (P("kgrp", "band", None, None), P("kgrp", None, None, None), P(), P(), P(), P())
    out_specs = P("band", "kgrp", None, None)
    body = functools.partial(shards, mesh.shape["kgrp"], mesh.shape["band"])
    return jax.shard_map(body, mesh=mesh, in_specs=in_specs, out_specs=out_specs, check_vma=False)
```

time: 904 us -> 825 us (0.913)
  waiting for transfers between devices: 400 us -> 0 us
  Pallas kernels: 394 us -> 754 us
  starting transfers between devices: 24.4 us -> 0 us
  local copies, waits for them, and re-layouts: 21.8 us -> 6.6 us
    pallas_call x11 -> x1, Pallas kernels: 394 us -> 754 us  [fused(): pl.pallas_call(functools.partial(fused_kernel, kgrp, band), in_specs=[sca...]
    all_to_all x5 -> x0, waiting for transfers between devices: 292 us -> none  [exchange(): lax.all_to_all(chunk, ('kgrp', 'band'), split_axis=0, concat_axis=0, tile...]
    ppermute x3 -> x0, waiting for transfers between devices: 107 us -> none  [shards(): arrived.append(lax.ppermute(held, 'kgrp', ring))]
    all_to_all x5 -> x0, starting transfers between devices: 21.3 us -> none  [exchange(): lax.all_to_all(chunk, ('kgrp', 'band'), split_axis=0, concat_axis=0, tile...]
  transfers between devices with their start and end apart: 8 -> 0, of which waited for: 7 -> 0; matrix products, arithmetic and copies ran while one was open for 2% -> 0% of each run, Pallas kernels for 38% -> 0%
where the time goes in v1:
time: 825 us; the launch traced here: 823 us
  Pallas kernels  754 us (91%)
  blocking collectives  60.7 us (7%)
    pallas_call x1, Pallas kernels, fused(): pl.pallas_call(functools.partial(fused_kernel, kgrp, band), in_specs=[sca...  754 us
    all_to_all x1, blocking collectives, shards(): lax.all_to_all(sums, ('kgrp', 'band'), split_axis=0, concat_axis=0, tiled...  60.7 us

profile of v1, /device:TPU:0, one launch (start us, length us, event | category | flops | bytes accessed | tf_op | source)
XLA Modules:
  0.0 823.1 jit_solution(7688649243870563168)
XLA Ops:
  0.0 0.0 copy-start
  0.0 1.4 gather_fusion
  1.4 0.0 copy-done
  1.5 0.6 gather_fusion.2
  2.0 1.8 gather_fusion.1
  3.8 0.7 broadcast_select_fusion.factor_ref
  4.5 0.7 broadcast_select_fusion.1.index_ref
  5.2 754.0 %fused.1 = (bf16[32,32,2,4,16,128]{5,4,3,2,1,0:T(8,128)(2,1)}, bf16[8,1024,128]{2,1,0:T(8,128)(2,1)}) custom-call(s32[8]{0:T(128)} %partner_ref.1, s32[2,4096]{1,0:T(2,128)} %broadcast_select_fusion.1.index_ref, f32[2,4096]{1,0:T(2,128)} %broadcast_select_fusion.factor_ref, bf16[2,16,128,4096]{3,2,1,0:T(8,128)(2,1)} %densities_ref.1, ...), custom_call_target="tpu_custom_call" | custom-call | tf_op jit(solution)/shard_map/fused/pallas_call | solution.py:207
  759.2 2.2 copy.8
  761.4 0.0 copy-start.1
  761.4 60.7 %all_to_all.5 = bf16[32,2,8,16,128]{4,3,2,1,0:T(8,128)(2,1)S(1)} all-to-all(bf16[32,2,8,16,128]{4,3,2,1,0:T(8,128)(2,1)S(1)} %bitcast.14), channel_id=1, replica_groups=mesh['kgrp'=4,'band'=8] {'kgrp','band'}, dimensions={0} | all-to-all | bytes 4194304 | tf_op jit(solution)/shard_map/all_to_all | solution.py:248
  822.1 0.3 convert_reduce_fusion
  822.4 0.6 copy.9
  823.1 0.0 copy-done.1
  (6 shorter events, 0.1 us)
Async XLA Ops:
  0.0 1.4 copy-start
  761.4 61.7 %copy-start.1 = (f32[64,4096]{1,0:T(8,128)S(1)}, f32[64,4096]{1,0:T(8,128)}, u32[]{:S(2)}) copy-start(f32[64,4096]{1,0:T(8,128)} %param.11) | copy-start | bytes 3145732

commit v2 on v1

--- a/solution.py
+++ b/solution.py
@@ -17,7 +17,9 @@
     kgrp, band, partner_ref, index_ref, factor_ref, densities_ref, amplitudes_ref,
     recv_ref, out_ref,
     turned, staged, slots, block, amps, total,
+    core_out, core_in, chip_out, chip_in, far_out, far_in,
     turn_sem, send_sem, recv_sem, amp_send, amp_recv, load_sem,
+    core_sent, core_came, chip_sent, chip_came, far_sent, far_came,
 ):
     devices = kgrp * band
     per_group, rows, width, g_all = densities_ref.shape
@@ -30,6 +32,12 @@
     vb = band * rows
     my_k, my_b = lax.axis_index("kgrp"), lax.axis_index("band")
     me = my_k * band + my_b
+    near_k, near_b = math.gcd(kgrp, 2), math.gcd(band, 2)
+    wide_k, wide_b = kgrp // near_k, band // near_b
+    my_x, my_c = my_k // near_k, lax.rem(my_k, near_k)
+    my_z, my_y = my_b // near_b, lax.rem(my_b, near_b)
+    half = wide_k * per_group
+    away = (near_k - 1) * half
 
     def peer(m):
         return lax.rem(my_k + lax.rem(m, kgrp), kgrp), lax.rem(my_b + m // kgrp, band)
@@ -98,6 +106,94 @@
         lax.fori_loop(1, devices, one, 0)
         pltpu.make_async_copy(piece(slots.at[slot, me]), piece(recv_ref.at[chunk, me]), send_sem.at[slot]).start()
 
+    def core_copy(r, step_c, order, to_c):
+        at = step_c - 1
+        core_out[at, order] = total[r].astype(core_out.dtype)
+        pltpu.make_async_remote_copy(
+            src_ref=core_out.at[at, order],
+            dst_ref=core_in.at[at, order],
+            send_sem=core_sent,
+            recv_sem=core_came.at[order],
+            device_id=(my_x * near_k + to_c, my_b),
+            device_id_type=MESH,
+        ).start()
+
+    def chip_copies(r, step_x, order, pair, to_x):
+        if near_k > 1:
+            came = core_in.at[:, order]
+            pltpu.make_async_copy(came, came, core_came.at[order]).wait()
+        for step_y in range(near_b):
+            to_y = lax.rem(my_y + step_y, near_b)
+            value = total[r, :, :, to_y]
+            for at in range(near_k - 1):
+                value = value + core_in[at, order, :, :, to_y].astype(jnp.float32)
+
+            def leave(value=value, step_y=step_y, to_y=to_y):
+                chip_out[order, step_y] = value.astype(chip_out.dtype)
+                pltpu.make_async_remote_copy(
+                    src_ref=chip_out.at[order, step_y],
+                    dst_ref=chip_in.at[pair, step_x * near_b + step_y - 1],
+                    send_sem=chip_sent,
+                    recv_sem=chip_came.at[pair],
+                    device_id=(to_x * near_k + my_c, my_z * near_b + to_y),
+                    device_id_type=MESH,
+                ).start()
+
+            def keep(value=value, to_y=to_y):
+                total[r, :, :, to_y] = value
+
+            if step_y:
+                leave()
+            else:
+                pl.when(step_x > 0)(leave)
+                pl.when(step_x == 0)(keep)
+
+    def finish():
+        own = [my_k * per_group + pair for pair in range(per_group)]
+        peers = wide_k * near_b - 1
+
+        def gathered(pair, z):
+            value = total[own[pair], :, z, my_y]
+            for at in range(peers):
+                value = value + chip_in[pair, at, :, z].astype(jnp.float32)
+            return value
+
+        for pair in range(per_group):
+            if peers:
+                pltpu.make_async_copy(chip_in.at[pair], chip_in.at[pair], chip_came.at[pair]).wait()
+
+            def one(step, carry, pair=pair):
+                to_z = lax.rem(my_z + step, wide_b)
+                far_out[pair, step - 1] = gathered(pair, to_z).astype(far_out.dtype)
+                pltpu.make_async_remote_copy(
+                    src_ref=far_out.at[pair, step - 1],
+                    dst_ref=far_in.at[pair, step - 1],
+                    send_sem=far_sent,
+                    recv_sem=far_came.at[pair],
+                    device_id=(my_k, to_z * near_b + my_y),
+                    device_id_type=MESH,
+                ).start()
+                return carry
+
+            lax.fori_loop(1, wide_b, one, 0)
+        for pair in range(per_group):
+            value = gathered(pair, my_z)
+            if wide_b > 1:
+                pltpu.make_async_copy(far_in.at[pair], far_in.at[pair], far_came.at[pair]).wait()
+            for at in range(wide_b - 1):
+                value = value + far_in[pair, at].astype(jnp.float32)
+            value = value * (1.0 / math.sqrt(g_all))
+            out_ref[:, pair] = jnp.swapaxes(value, 0, 1).astype(out_ref.dtype)
+        if near_k > 1:
+            pltpu.make_async_copy(core_out, core_out, core_sent).wait()
+        for order in range(half):
+            for step_y in range(near_b):
+                if step_y or order < half - per_group:
+                    sent = chip_out.at[order, step_y]
+                    pltpu.make_async_copy(sent, sent, chip_sent).wait()
+        if wide_b > 1:
+            pltpu.make_async_copy(far_out, far_out, far_sent).wait()
+
     def ladder(chunk):
         others = pl.ds(0, devices - 1)
         pltpu.make_async_copy(
@@ -107,7 +203,11 @@
         load.start()
         load.wait()
 
-        def one(r, carry):
+        def one(i, carry):
+            order = lax.rem(i, half)
+            step_c, step_x, pair = near_k - 1 - i // half, wide_k - 1 - order // per_group, lax.rem(order, per_group)
+            to_c, to_x = lax.rem(my_c + step_c, near_k), lax.rem(my_x + step_x, wide_k)
+            r = (to_x * near_k + to_c) * per_group + pair
             q = partner_ref[r]
             left_base, left_pair = r // per_group * band, lax.rem(r, per_group)
             right_base, right_pair = q // per_group * band, lax.rem(q, per_group)
@@ -132,7 +232,17 @@
                 ],
                 axis=0,
             )
-            total[r] += lax.dot_general(wide, right, (((1,), (1,)), ((), ())), preferred_element_type=jnp.float32)
+            part = lax.dot_general(wide, right, (((1,), (1,)), ((), ())), preferred_element_type=jnp.float32)
+            total[r] += part.reshape(slabs, wide_b, near_b, rows, vb)
+
+            @pl.when((chunk == chunks - 1) & (i < away))
+            def _():
+                core_copy(r, step_c, order, to_c)
+
+            @pl.when((chunk == chunks - 1) & (i >= away))
+            def _():
+                chip_copies(r, step_x, order, pair, to_x)
+
             return carry
 
         lax.fori_loop(0, pairs, one, 0)
@@ -187,7 +297,7 @@
         return carry
 
     lax.fori_loop(SLOTS, chunks + SLOTS, main, 0)
-    out_ref[...] = total[...].astype(out_ref.dtype)
+    finish()
 
 
 def fused(kgrp, band, densities, amplitudes, partner, index, factors):
@@ -204,13 +314,17 @@
     anywhere = pl.BlockSpec(memory_space=pl.ANY)
     scalars = pl.BlockSpec(memory_space=pltpu.SMEM)
     piece = (per_group, depth, rows, width)
+    near_k, near_b = math.gcd(kgrp, 2), math.gcd(band, 2)
+    wide_k, wide_b = kgrp // near_k, band // near_b
+    half = wide_k * per_group
+    spread = (slabs, wide_b, near_b, rows, vb)
     return pl.pallas_call(
         functools.partial(fused_kernel, kgrp, band),
         in_specs=[scalars, scalars, scalars, anywhere, anywhere],
         out_specs=[anywhere, pl.BlockSpec(memory_space=pltpu.VMEM)],
         out_shape=[
             jax.ShapeDtypeStruct((chunks, devices) + piece, kind),
-            jax.ShapeDtypeStruct((pairs, slabs * vb, vb), kind),
+            jax.ShapeDtypeStruct((rows, per_group, slabs, vb), kind),
         ],
         scratch_shapes=[
             pltpu.VMEM((per_group * g_all // span, span, rows, width), kind),
@@ -218,13 +332,25 @@
             pltpu.VMEM((SLOTS, devices) + piece, kind),
             pltpu.VMEM((devices,) + piece, kind),
             pltpu.VMEM((pairs,) + amplitudes.shape[1:], kind),
-            pltpu.VMEM((pairs, slabs * vb, vb), jnp.float32),
+            pltpu.VMEM((pairs,) + spread, jnp.float32),
+            pltpu.VMEM((max(near_k - 1, 1), half) + spread, kind),
+            pltpu.VMEM((max(near_k - 1, 1), half) + spread, kind),
+            pltpu.VMEM((half, near_b, slabs, wide_b, rows, vb), kind),
+            pltpu.VMEM((per_group, max(wide_k * near_b - 1, 1), slabs, wide_b, rows, vb), kind),
+            pltpu.VMEM((per_group, max(wide_b - 1, 1), slabs, rows, vb), kind),
+            pltpu.VMEM((per_group, max(wide_b - 1, 1), slabs, rows, vb), kind),
             pltpu.SemaphoreType.DMA((2,)),
             pltpu.SemaphoreType.DMA((SLOTS,)),
             pltpu.SemaphoreType.DMA((chunks,)),
             pltpu.SemaphoreType.DMA,
             pltpu.SemaphoreType.DMA,
             pltpu.SemaphoreType.DMA,
+            pltpu.SemaphoreType.DMA,
+            pltpu.SemaphoreType.DMA((half,)),
+            pltpu.SemaphoreType.DMA,
+            pltpu.SemaphoreType.DMA((per_group,)),
+            pltpu.SemaphoreType.DMA,
+            pltpu.SemaphoreType.DMA((per_group,)),
         ],
         compiler_params=pltpu.CompilerParams(
             collective_id=0, has_side_effects=True, vmem_limit_bytes=62 * 1024 * 1024
@@ -234,20 +360,12 @@
 
 
 def shards(kgrp, band, densities, amplitudes, partner, qtable, grid_map, coulomb):
-    per_group, rows, width, g_all = densities.shape
-    slabs = amplitudes.shape[1]
-    vb = rows * band
-    devices = kgrp * band
+    per_group = densities.shape[0]
     own_ids = lax.axis_index("kgrp") * per_group + jnp.arange(per_group, dtype=jnp.int32)
     transfers = jnp.take(qtable, own_ids)
     index = jnp.take(grid_map, transfers, axis=0)
     factors = jnp.take(coulomb, transfers, axis=0)
-    _, sums = fused(kgrp, band, densities, amplitudes, partner, index, factors)
-    sums = sums.reshape(kgrp, per_group, slabs, band, rows, vb)
-    sums = jnp.transpose(sums, (0, 3, 1, 2, 4, 5)).reshape(devices, per_group, slabs, rows, vb)
-    sums = lax.all_to_all(sums, ("kgrp", "band"), split_axis=0, concat_axis=0, tiled=True)
-    summed = jnp.sum(sums.astype(jnp.float32), axis=0) * (1.0 / math.sqrt(g_all))
-    return jnp.transpose(summed, (2, 0, 1, 3)).astype(jnp.bfloat16)
+    return fused(kgrp, band, densities, amplitudes, partner, index, factors)[1]
 
 
 def solution(mesh):

time: 825 us -> 786 us (0.953)
  blocking collectives: 60.7 us -> 0 us
  Pallas kernels: 754 us -> 778 us
    all_to_all x1 -> x0, blocking collectives: 60.7 us -> none  [shards(): lax.all_to_all(sums, ('kgrp', 'band'), split_axis=0, concat_axis=0, tiled...]
    pallas_call x1, Pallas kernels: 754 us -> 778 us  [fused(): pl.pallas_call(functools.partial(fused_kernel, kgrp, band), in_specs=[sca...]
where the time goes in v2:
time: 786 us; the launch traced here: 784 us
  Pallas kernels  778 us (99%)
    pallas_call x1, Pallas kernels, fused(): pl.pallas_call(functools.partial(fused_kernel, kgrp, band), in_specs=[sca...  778 us

profile of v2, /device:TPU:0, one launch (start us, length us, event | category | flops | bytes accessed | tf_op | source)
XLA Modules:
  0.0 784.2 jit_solution(10025997038429957272)
XLA Ops:
  0.0 0.0 copy-start
  0.0 1.4 gather_fusion
  1.4 0.0 copy-done
  1.5 0.6 gather_fusion.2
  2.0 0.7 broadcast_select_fusion.factor_ref
  2.7 1.8 gather_fusion.1
  4.5 0.7 broadcast_select_fusion.1.index_ref
  5.2 777.5 %fused.1 = (bf16[32,32,2,4,16,128]{5,4,3,2,1,0:T(8,128)(2,1)}, bf16[16,2,8,128]{3,2,1,0:T(8,128)(2,1)}) custom-call(s32[8]{0:T(128)} %partner_ref.1, s32[2,4096]{1,0:T(2,128)} %broadcast_select_fusion.1.index_ref, f32[2,4096]{1,0:T(2,128)} %broadcast_select_fusion.factor_ref, bf16[2,16,128,4096]{3,2,1,0:T(8,128)(2,1)} %densities_ref.1, ...), custom_call_target="tpu_custom_call" | custom-call | tf_op jit(solution)/shard_map/fused/pallas_call | solution.py:321
  782.8 1.5 copy.8
  (5 shorter events, 0.0 us)
Async XLA Ops:
  0.0 1.4 copy-start

commit v3 on v2

--- a/solution.py
+++ b/solution.py
@@ -11,19 +11,22 @@
 MESH = pl.DeviceIdType.MESH
 SLOTS = 3
 DEPTH = 4
+STAGES = 4
 
 
 def fused_kernel(
-    kgrp, band, partner_ref, index_ref, factor_ref, densities_ref, amplitudes_ref,
+    kgrp, band, partner_ref, qtable_ref, densities_ref, amplitudes_ref, grid_ref, coulomb_ref,
     recv_ref, out_ref,
+    grids, kernels, index_rows, factor_rows, index_ref, factor_ref,
     turned, staged, slots, block, amps, total,
     core_out, core_in, chip_out, chip_in, far_out, far_in,
-    turn_sem, send_sem, recv_sem, amp_send, amp_recv, load_sem,
+    table_sem, turn_sem, send_sem, recv_sem, amp_send, amp_recv, load_sem,
     core_sent, core_came, chip_sent, chip_came, far_sent, far_came,
 ):
     devices = kgrp * band
     per_group, rows, width, g_all = densities_ref.shape
-    rows_by_g = turned.reshape(per_group * g_all, rows, width)
+    split, part_rows = turned.shape[2:4]
+    rows_by_g = turned.reshape(per_group * g_all, split, part_rows, width)
     chunks = recv_ref.shape[0]
     depth = slots.shape[3]
     slabs = amps.shape[1]
@@ -42,6 +45,33 @@
     def peer(m):
         return lax.rem(my_k + lax.rem(m, kgrp), kgrp), lax.rem(my_b + m // kgrp, band)
 
+    span = staged.shape[-1]
+    steps = g_all // span
+
+    def fetch(p, h, i):
+        return pltpu.make_async_copy(
+            densities_ref.at[
+                p,
+                pl.ds(h * part_rows, part_rows),
+                :,
+                pl.ds(pl.multiple_of(i * span, span), span),
+            ],
+            staged.at[lax.rem(i, STAGES)],
+            turn_sem.at[lax.rem(i, STAGES)],
+        )
+
+    def fetch_first(p, h):
+        for i in range(STAGES - 1):
+            fetch(p, h, i).start()
+
+    tables = [
+        pltpu.make_async_copy(grid_ref, grids, table_sem.at[0]),
+        pltpu.make_async_copy(coulomb_ref, kernels, table_sem.at[1]),
+    ]
+    for copy in tables:
+        copy.start()
+    fetch_first(0, 0)
+
     barrier = pltpu.get_barrier_semaphore()
 
     def greet(m, carry):
@@ -49,41 +79,44 @@
         return carry
 
     lax.fori_loop(1, devices, greet, 0)
+    for copy in tables:
+        copy.wait()
+    for p in range(per_group):
+        transfer = qtable_ref[my_k * per_group + p]
+        index_rows[p] = grids[transfer]
+        factor_rows[p] = kernels[transfer]
+    tables = [
+        pltpu.make_async_copy(index_rows, index_ref, table_sem.at[0]),
+        pltpu.make_async_copy(factor_rows, factor_ref, table_sem.at[1]),
+    ]
+    for copy in tables:
+        copy.start()
     pl.semaphore_wait(barrier, devices - 1)
-
-    span = staged.shape[-1]
-    steps = g_all // span
-
-    def fetch(p, i):
-        return pltpu.make_async_copy(
-            densities_ref.at[p, :, :, pl.ds(pl.multiple_of(i * span, span), span)],
-            staged.at[lax.rem(i, 2)],
-            turn_sem.at[lax.rem(i, 2)],
-        )
-
-    def turn(p):
-        fetch(p, 0).start()
-
+    for copy in tables:
+        copy.wait()
+
+    def turn(p, h):
         def one(i, carry):
-            @pl.when(i + 1 < steps)
+            @pl.when(i + STAGES - 1 < steps)
             def _():
-                fetch(p, i + 1).start()
-
-            fetch(p, i).wait()
-            flat = staged[lax.rem(i, 2)].reshape(rows * width, span)
-            turned[p * steps + i] = flat.T.reshape(span, rows, width)
+                fetch(p, h, i + STAGES - 1).start()
+
+            fetch(p, h, i).wait()
+            flat = staged[lax.rem(i, STAGES)].reshape(part_rows * width, span)
+            turned[p * steps + i, :, h] = flat.T.reshape(span, part_rows, width)
             return carry
 
         lax.fori_loop(0, steps, one, 0)
 
-    def pick(p, chunk):
+    def pick(p, chunk, *part):
         slot = lax.rem(chunk, SLOTS)
 
         def one(d, carry):
             first = d * g_shard + chunk * depth
             for j in range(depth):
-                row = rows_by_g[p * g_all + index_ref[p, first + j]].astype(jnp.float32) * factor_ref[p, first + j]
-                slots[slot, d, p, j] = row.astype(slots.dtype)
+                source = (p * g_all + index_ref[p, first + j],) + part
+                row = rows_by_g[source].astype(jnp.float32) * factor_ref[p, first + j]
+                slots[(slot, d, p, j) + part] = row.astype(slots.dtype)
             return carry
 
         lax.fori_loop(0, devices, one, 0, unroll=2)
@@ -212,11 +245,13 @@
             left_base, left_pair = r // per_group * band, lax.rem(r, per_group)
             right_base, right_pair = q // per_group * band, lax.rem(q, per_group)
             left = jnp.concatenate(
-                [block[left_base + b, left_pair, j] for j in range(depth) for b in range(band)], axis=0
+                [block[left_base + b, left_pair, j].reshape(rows, width) for j in range(depth) for b in range(band)], axis=0
             )
             right = jnp.concatenate(
                 [
-                    jnp.concatenate([block[right_base + b, right_pair, j] for b in range(band)], axis=0)
+                    jnp.concatenate(
+                        [block[right_base + b, right_pair, j].reshape(rows, width) for b in range(band)], axis=0
+                    )
                     for j in range(depth)
                 ],
                 axis=1,
@@ -261,12 +296,17 @@
     own_amp = pltpu.make_async_copy(amplitudes_ref, amps.at[pl.ds(my_k * per_group, per_group)], load_sem)
 
     def begin(p, carry):
-        turn(p)
-        for chunk in range(SLOTS):
-            pick(p, chunk)
-            if chunk:
-                send(chunk - 1, lambda ref: ref.at[p])
-        send(SLOTS - 1, lambda ref: ref.at[p])
+        for h in range(split):
+            turn(p, h)
+            if h + 1 < split:
+                fetch_first(p, h + 1)
+            else:
+                pl.when(p + 1 < per_group)(functools.partial(fetch_first, p + 1, 0))
+            for chunk in range(SLOTS):
+                pick(p, chunk, h)
+                if chunk:
+                    send(chunk - 1, lambda ref: ref.at[p, :, h])
+            send(SLOTS - 1, lambda ref: ref.at[p, :, h])
         return carry
 
     total[...] = jnp.zeros_like(total)
@@ -300,7 +340,7 @@
     finish()
 
 
-def fused(kgrp, band, densities, amplitudes, partner, index, factors):
+def fused(kgrp, band, densities, amplitudes, partner, qtable, grid_map, coulomb):
     per_group, rows, width, g_all = densities.shape
     slabs = amplitudes.shape[1]
     devices = kgrp * band
@@ -313,22 +353,30 @@
     kind = densities.dtype
     anywhere = pl.BlockSpec(memory_space=pl.ANY)
     scalars = pl.BlockSpec(memory_space=pltpu.SMEM)
-    piece = (per_group, depth, rows, width)
+    split = math.gcd(max(rows // 8, 1), 2)
+    part_rows = rows // split
+    piece = (per_group, depth, split, part_rows, width)
     near_k, near_b = math.gcd(kgrp, 2), math.gcd(band, 2)
     wide_k, wide_b = kgrp // near_k, band // near_b
     half = wide_k * per_group
     spread = (slabs, wide_b, near_b, rows, vb)
     return pl.pallas_call(
         functools.partial(fused_kernel, kgrp, band),
-        in_specs=[scalars, scalars, scalars, anywhere, anywhere],
+        in_specs=[scalars, scalars, anywhere, anywhere, anywhere, anywhere],
         out_specs=[anywhere, pl.BlockSpec(memory_space=pltpu.VMEM)],
         out_shape=[
             jax.ShapeDtypeStruct((chunks, devices) + piece, kind),
             jax.ShapeDtypeStruct((rows, per_group, slabs, vb), kind),
         ],
         scratch_shapes=[
-            pltpu.VMEM((per_group * g_all // span, span, rows, width), kind),
-            pltpu.VMEM((2, rows, width, span), kind),
+            pltpu.VMEM(grid_map.shape, grid_map.dtype),
+            pltpu.VMEM(coulomb.shape, coulomb.dtype),
+            pltpu.VMEM((per_group, g_all), grid_map.dtype),
+            pltpu.VMEM((per_group, g_all), coulomb.dtype),
+            pltpu.SMEM((per_group, g_all), grid_map.dtype),
+            pltpu.SMEM((per_group, g_all), coulomb.dtype),
+            pltpu.VMEM((per_group * g_all // span, span, split, part_rows, width), kind),
+            pltpu.VMEM((STAGES, part_rows, width, span), kind),
             pltpu.VMEM((SLOTS, devices) + piece, kind),
             pltpu.VMEM((devices,) + piece, kind),
             pltpu.VMEM((pairs,) + amplitudes.shape[1:], kind),
@@ -340,6 +388,7 @@
             pltpu.VMEM((per_group, max(wide_b - 1, 1), slabs, rows, vb), kind),
             pltpu.VMEM((per_group, max(wide_b - 1, 1), slabs, rows, vb), kind),
             pltpu.SemaphoreType.DMA((2,)),
+            pltpu.SemaphoreType.DMA((STAGES,)),
             pltpu.SemaphoreType.DMA((SLOTS,)),
             pltpu.SemaphoreType.DMA((chunks,)),
             pltpu.SemaphoreType.DMA,
@@ -356,16 +405,11 @@
             collective_id=0, has_side_effects=True, vmem_limit_bytes=62 * 1024 * 1024
         ),
         name="fused",
-    )(partner, index, factors, densities, amplitudes)
+    )(partner, qtable, densities, amplitudes, grid_map, coulomb)
 
 
 def shards(kgrp, band, densities, amplitudes, partner, qtable, grid_map, coulomb):
-    per_group = densities.shape[0]
-    own_ids = lax.axis_index("kgrp") * per_group + jnp.arange(per_group, dtype=jnp.int32)
-    transfers = jnp.take(qtable, own_ids)
-    index = jnp.take(grid_map, transfers, axis=0)
-    factors = jnp.take(coulomb, transfers, axis=0)
-    return fused(kgrp, band, densities, amplitudes, partner, index, factors)[1]
+    return fused(kgrp, band, densities, amplitudes, partner, qtable, grid_map, coulomb)[1]
 
 
 def solution(mesh):

time: 786 us -> 779 us (level)
  no operation moved by 1% of the time
where the time goes in v3:
time: 779 us; the launch traced here: 777 us
  Pallas kernels  775 us (99%)
    pallas_call x1, Pallas kernels, fused(): pl.pallas_call(functools.partial(fused_kernel, kgrp, band), in_specs=[sca...  775 us

profile of v3, /device:TPU:0, one launch (start us, length us, event | category | flops | bytes accessed | tf_op | source)
XLA Modules:
  0.0 776.9 jit_solution(8285479309021518016)
XLA Ops:
  0.0 775.4 %fused.1 = (bf16[32,32,2,4,2,8,128]{6,5,4,3,2,1,0:T(8,128)(2,1)}, bf16[16,2,8,128]{3,2,1,0:T(8,128)(2,1)}) custom-call(s32[8]{0:T(128)} %partner_ref.1, s32[8]{0:T(128)} %qtable_ref.1, bf16[2,16,128,4096]{3,2,1,0:T(8,128)(2,1)} %densities_ref.1, bf16[2,8,128,128]{3,2,1,0:T(8,128)(2,1)} %amplitudes_ref.1, s32[64,4096]{1,0:T(8,128)} %grid_ref.1, ...), custom_call_target="tpu_custom_call" | custom-call | tf_op jit(solution)/shard_map/fused/pallas_call | solution.py:363
  775.4 1.5 copy.8

commit v4 on v3

--- a/solution.py
+++ b/solution.py
@@ -9,9 +9,10 @@
 from jax.sharding import PartitionSpec as P
 
 MESH = pl.DeviceIdType.MESH
-SLOTS = 3
+SLOTS = 6
 DEPTH = 4
 STAGES = 4
+LAG = 2
 
 
 def fused_kernel(
@@ -28,7 +29,7 @@
     split, part_rows = turned.shape[2:4]
     rows_by_g = turned.reshape(per_group * g_all, split, part_rows, width)
     chunks = recv_ref.shape[0]
-    depth = slots.shape[3]
+    ahead, depth = slots.shape[0], slots.shape[3]
     slabs = amps.shape[1]
     g_shard = chunks * depth
     pairs = kgrp * per_group
@@ -108,36 +109,67 @@
 
         lax.fori_loop(0, steps, one, 0)
 
-    def pick(p, chunk, *part):
-        slot = lax.rem(chunk, SLOTS)
-
+    def pick(p, chunk, d, *part):
+        slot, first = lax.rem(chunk, ahead), d * g_shard + chunk * depth
+        for j in range(depth):
+            source = (p * g_all + index_ref[p, first + j],) + part
+            row = rows_by_g[source].astype(jnp.float32) * factor_ref[p, first + j]
+            slots[(slot, d, p, j) + part] = row.astype(slots.dtype)
+
+    def pick_all(p, chunk):
         def one(d, carry):
-            first = d * g_shard + chunk * depth
-            for j in range(depth):
-                source = (p * g_all + index_ref[p, first + j],) + part
-                row = rows_by_g[source].astype(jnp.float32) * factor_ref[p, first + j]
-                slots[(slot, d, p, j) + part] = row.astype(slots.dtype)
+            pick(p, chunk, d)
             return carry
 
         lax.fori_loop(0, devices, one, 0, unroll=2)
 
-    def send(chunk, piece):
-        slot = lax.rem(chunk, SLOTS)
-
+    def send(chunk, m, piece):
+        slot = lax.rem(chunk, ahead)
+        to_k, to_b = peer(m)
+        pltpu.make_async_remote_copy(
+            src_ref=piece(slots.at[slot, to_k * band + to_b]),
+            dst_ref=piece(recv_ref.at[chunk, me]),
+            send_sem=send_sem.at[slot],
+            recv_sem=recv_sem.at[chunk],
+            device_id=(to_k, to_b),
+            device_id_type=MESH,
+        ).start()
+
+    def put(chunk, piece):
+        slot = lax.rem(chunk, ahead)
+        pltpu.make_async_copy(piece(slots.at[slot, me]), piece(recv_ref.at[chunk, me]), send_sem.at[slot]).start()
+
+    def send_all(chunk):
         def one(m, carry):
-            to_k, to_b = peer(m)
-            pltpu.make_async_remote_copy(
-                src_ref=piece(slots.at[slot, to_k * band + to_b]),
-                dst_ref=piece(recv_ref.at[chunk, me]),
-                send_sem=send_sem.at[slot],
-                recv_sem=recv_sem.at[chunk],
-                device_id=(to_k, to_b),
-                device_id_type=MESH,
-            ).start()
+            send(chunk, m, lambda ref: ref)
             return carry
 
         lax.fori_loop(1, devices, one, 0)
-        pltpu.make_async_copy(piece(slots.at[slot, me]), piece(recv_ref.at[chunk, me]), send_sem.at[slot]).start()
+        put(chunk, lambda ref: ref)
+
+    def pick_and_send(p, h, chunk):
+        def piece(ref):
+            return ref.at[p, :, h]
+
+        def turned_to(i):
+            return lax.rem(i + devices // 2, devices)
+
+        def one(i, carry):
+            @pl.when(i < devices)
+            def _():
+                to_k, to_b = peer(turned_to(i))
+                pick(p, chunk, to_k * band + to_b, h)
+
+            m = turned_to(i + devices - LAG)
+
+            @pl.when((i >= LAG) & (m > 0))
+            def _():
+                send(chunk, m, piece)
+
+            return carry
+
+        lax.fori_loop(0, devices + LAG, one, 0)
+        put(chunk, piece)
 
     def core_copy(r, step_c, order, to_c):
         at = step_c - 1
@@ -302,11 +334,12 @@
                 fetch_first(p, h + 1)
             else:
                 pl.when(p + 1 < per_group)(functools.partial(fetch_first, p + 1, 0))
-            for chunk in range(SLOTS):
-                pick(p, chunk, h)
-                if chunk:
-                    send(chunk - 1, lambda ref: ref.at[p, :, h])
-            send(SLOTS - 1, lambda ref: ref.at[p, :, h])
+
+            def one(chunk, inner, h=h):
+                pick_and_send(p, h, chunk)
+                return inner
+
+            lax.fori_loop(0, ahead, one, 0)
         return carry
 
     total[...] = jnp.zeros_like(total)
@@ -320,23 +353,23 @@
     pltpu.make_async_copy(all_amps, all_amps, amp_recv).wait()
 
     def main(chunk, carry):
-        slot = lax.rem(chunk, SLOTS)
+        slot = lax.rem(chunk, ahead)
         pltpu.make_async_copy(slots.at[slot], slots.at[slot], send_sem.at[slot]).wait()
 
         @pl.when(chunk < chunks)
         def _():
             for p in range(per_group):
-                pick(p, chunk)
-
-        ladder(chunk - SLOTS)
+                pick_all(p, chunk)
+
+        ladder(chunk - ahead)
 
         @pl.when(chunk < chunks)
         def _():
-            send(chunk, lambda ref: ref)
+            send_all(chunk)
 
         return carry
 
-    lax.fori_loop(SLOTS, chunks + SLOTS, main, 0)
+    lax.fori_loop(ahead, chunks + ahead, main, 0)
     finish()
 
 
@@ -349,6 +382,7 @@
     g_shard = g_all // devices
     depth = math.gcd(g_shard, DEPTH)
     chunks = g_shard // depth
+    ahead = min(SLOTS, chunks)
     span = math.gcd(g_all, 256)
     kind = densities.dtype
     anywhere = pl.BlockSpec(memory_space=pl.ANY)
@@ -377,7 +411,7 @@
             pltpu.SMEM((per_group, g_all), coulomb.dtype),
             pltpu.VMEM((per_group * g_all // span, span, split, part_rows, width), kind),
             pltpu.VMEM((STAGES, part_rows, width, span), kind),
-            pltpu.VMEM((SLOTS, devices) + piece, kind),
+            pltpu.VMEM((ahead, devices) + piece, kind),
             pltpu.VMEM((devices,) + piece, kind),
             pltpu.VMEM((pairs,) + amplitudes.shape[1:], kind),
             pltpu.VMEM((pairs,) + spread, jnp.float32),
@@ -389,7 +423,7 @@
             pltpu.VMEM((per_group, max(wide_b - 1, 1), slabs, rows, vb), kind),
             pltpu.SemaphoreType.DMA((2,)),
             pltpu.SemaphoreType.DMA((STAGES,)),
-            pltpu.SemaphoreType.DMA((SLOTS,)),
+            pltpu.SemaphoreType.DMA((ahead,)),
             pltpu.SemaphoreType.DMA((chunks,)),
             pltpu.SemaphoreType.DMA,
             pltpu.SemaphoreType.DMA,
@@ -402,7 +436,7 @@
             pltpu.SemaphoreType.DMA((per_group,)),
         ],
         compiler_params=pltpu.CompilerParams(
-            collective_id=0, has_side_effects=True, vmem_limit_bytes=62 * 1024 * 1024
+            collective_id=0, has_side_effects=True, vmem_limit_bytes=63 * 1024 * 1024
         ),
         name="fused",
     )(partner, qtable, densities, amplitudes, grid_map, coulomb)

time: 779 us -> 767 us (0.985)
  Pallas kernels: 775 us -> 764 us
    pallas_call x1, Pallas kernels: 775 us -> 764 us  [fused(): pl.pallas_call(functools.partial(fused_kernel, kgrp, band), in_specs=[sca...]
where the time goes in v4:
time: 767 us; the launch traced here: 766 us
  Pallas kernels  764 us (100%)
    pallas_call x1, Pallas kernels, fused(): pl.pallas_call(functools.partial(fused_kernel, kgrp, band), in_specs=[sca...  764 us

profile of v4, /device:TPU:0, one launch (start us, length us, event | category | flops | bytes accessed | tf_op | source)
XLA Modules:
  0.0 765.6 jit_solution(6679237231543502371)
XLA Ops:
  0.0 764.1 %fused.1 = (bf16[32,32,2,4,2,8,128]{6,5,4,3,2,1,0:T(8,128)(2,1)}, bf16[16,2,8,128]{3,2,1,0:T(8,128)(2,1)}) custom-call(s32[8]{0:T(128)} %partner_ref.1, s32[8]{0:T(128)} %qtable_ref.1, bf16[2,16,128,4096]{3,2,1,0:T(8,128)(2,1)} %densities_ref.1, bf16[2,8,128,128]{3,2,1,0:T(8,128)(2,1)} %amplitudes_ref.1, s32[64,4096]{1,0:T(8,128)} %grid_ref.1, ...), custom_call_target="tpu_custom_call" | custom-call | tf_op jit(solution)/shard_map/fused/pallas_call | solution.py:397
  764.1 1.5 copy.8

commit v5 on v4

--- a/solution.py
+++ b/solution.py
@@ -9,7 +9,7 @@
 from jax.sharding import PartitionSpec as P
 
 MESH = pl.DeviceIdType.MESH
-SLOTS = 6
+SLOTS = 7
 DEPTH = 4
 STAGES = 4
 LAG = 2
@@ -92,9 +92,6 @@
     ]
     for copy in tables:
         copy.start()
-    pl.semaphore_wait(barrier, devices - 1)
-    for copy in tables:
-        copy.wait()
 
     def turn(p, h):
         def one(i, carry):
@@ -123,14 +120,14 @@
 
         lax.fori_loop(0, devices, one, 0, unroll=2)
 
-    def send(chunk, m, piece):
+    def send(chunk, m, piece, came=None):
         slot = lax.rem(chunk, ahead)
         to_k, to_b = peer(m)
         pltpu.make_async_remote_copy(
             src_ref=piece(slots.at[slot, to_k * band + to_b]),
             dst_ref=piece(recv_ref.at[chunk, me]),
             send_sem=send_sem.at[slot],
-            recv_sem=recv_sem.at[chunk],
+            recv_sem=recv_sem.at[chunk if came is None else came],
             device_id=(to_k, to_b),
             device_id_type=MESH,
         ).start()
@@ -139,13 +136,19 @@
         slot = lax.rem(chunk, ahead)
         pltpu.make_async_copy(piece(slots.at[slot, me]), piece(recv_ref.at[chunk, me]), send_sem.at[slot]).start()
 
-    def send_all(chunk):
+    def send_all(chunk, piece, came=None):
         def one(m, carry):
-            send(chunk, m, lambda ref: ref)
+            send(chunk, m, piece, came)
             return carry
 
         lax.fori_loop(1, devices, one, 0)
-        put(chunk, lambda ref: ref)
+        put(chunk, piece)
+
+    def head_of(ref):
+        return ref.at[:, pl.ds(0, depth - 1)]
+
+    def tail_of(ref):
+        return ref.at[:, pl.ds(depth - 1, 1)]
 
     def pick_and_send(p, h, chunk):
         def piece(ref):
@@ -259,12 +262,11 @@
         if wide_b > 1:
             pltpu.make_async_copy(far_out, far_out, far_sent).wait()
 
-    def ladder(chunk):
-        others = pl.ds(0, devices - 1)
-        pltpu.make_async_copy(
-            recv_ref.at[chunk, others], recv_ref.at[chunk, others], recv_sem.at[chunk]
-        ).wait()
-        load = pltpu.make_async_copy(recv_ref.at[chunk], block, load_sem)
+    def ladder(chunk, first=0, count=depth, came=None, last=False):
+        window = (slice(None), slice(None), pl.ds(first, count))
+        others = recv_ref.at[(chunk, pl.ds(0, devices - 1)) + window[1:]]
+        pltpu.make_async_copy(others, others, recv_sem.at[chunk if came is None else came]).wait()
+        load = pltpu.make_async_copy(recv_ref.at[(chunk,) + window], block.at[window], load_sem)
         load.start()
         load.wait()
 
@@ -277,14 +279,14 @@
             left_base, left_pair = r // per_group * band, lax.rem(r, per_group)
             right_base, right_pair = q // per_group * band, lax.rem(q, per_group)
             left = jnp.concatenate(
-                [block[left_base + b, left_pair, j].reshape(rows, width) for j in range(depth) for b in range(band)], axis=0
+                [block[left_base + b, left_pair, j].reshape(rows, width) for j in range(first, first + count) for b in range(band)], axis=0
             )
             right = jnp.concatenate(
                 [
                     jnp.concatenate(
                         [block[right_base + b, right_pair, j].reshape(rows, width) for b in range(band)], axis=0
                     )
-                    for j in range(depth)
+                    for j in range(first, first + count)
                 ],
                 axis=1,
             )
@@ -293,7 +295,7 @@
             wide = jnp.concatenate(
                 [
                     jnp.concatenate(
-                        [mixed[j * vb:(j + 1) * vb, s * width:(s + 1) * width] for j in range(depth)], axis=1
+                        [mixed[j * vb:(j + 1) * vb, s * width:(s + 1) * width] for j in range(count)], axis=1
                     )
                     for s in range(slabs)
                 ],
@@ -302,13 +304,9 @@
             part = lax.dot_general(wide, right, (((1,), (1,)), ((), ())), preferred_element_type=jnp.float32)
             total[r] += part.reshape(slabs, wide_b, near_b, rows, vb)
 
-            @pl.when((chunk == chunks - 1) & (i < away))
-            def _():
-                core_copy(r, step_c, order, to_c)
-
-            @pl.when((chunk == chunks - 1) & (i >= away))
-            def _():
-                chip_copies(r, step_x, order, pair, to_x)
+            if last:
+                pl.when(i < away)(lambda: core_copy(r, step_c, order, to_c))
+                pl.when(i >= away)(lambda: chip_copies(r, step_x, order, pair, to_x))
 
             return carry
 
@@ -329,7 +327,10 @@
 
     def begin(p, carry):
         for h in range(split):
-            turn(p, h)
+            if h:
+                turn(p, h)
+            else:
+                pl.when(p > 0)(functools.partial(turn, p, h))
             if h + 1 < split:
                 fetch_first(p, h + 1)
             else:
@@ -343,6 +344,10 @@
         return carry
 
     total[...] = jnp.zeros_like(total)
+    turn(0, 0)
+    for copy in tables:
+        copy.wait()
+    pl.semaphore_wait(barrier, devices - 1)
     lax.fori_loop(0, per_group, begin, 0)
     own_amp.start()
     for m in range(1, kgrp):
@@ -352,9 +357,12 @@
     pltpu.make_async_copy(all_amps, all_amps, amp_send).wait()
     pltpu.make_async_copy(all_amps, all_amps, amp_recv).wait()
 
-    def main(chunk, carry):
+    def freed(chunk):
         slot = lax.rem(chunk, ahead)
         pltpu.make_async_copy(slots.at[slot], slots.at[slot], send_sem.at[slot]).wait()
+
+    def main(chunk, carry):
+        freed(chunk)
 
         @pl.when(chunk < chunks)
         def _():
@@ -363,13 +371,21 @@
 
         ladder(chunk - ahead)
 
-        @pl.when(chunk < chunks)
+        @pl.when(chunk < chunks - 1)
         def _():
-            send_all(chunk)
+            send_all(chunk, lambda ref: ref)
+
+        @pl.when(chunk == chunks - 1)
+        def _():
+            send_all(chunk, head_of)
+            send_all(chunk, tail_of, chunks)
 
         return carry
 
-    lax.fori_loop(ahead, chunks + ahead, main, 0)
+    lax.fori_loop(ahead, chunks + ahead - 1, main, 0)
+    freed(chunks - 1)
+    ladder(chunks - 1, 0, depth - 1)
+    ladder(chunks - 1, depth - 1, 1, chunks, True)
     finish()
 
 
@@ -382,7 +398,7 @@
     g_shard = g_all // devices
     depth = math.gcd(g_shard, DEPTH)
     chunks = g_shard // depth
-    ahead = min(SLOTS, chunks)
+    ahead = min(SLOTS, chunks - 1)
     span = math.gcd(g_all, 256)
     kind = densities.dtype
     anywhere = pl.BlockSpec(memory_space=pl.ANY)
@@ -424,7 +440,7 @@
             pltpu.SemaphoreType.DMA((2,)),
             pltpu.SemaphoreType.DMA((STAGES,)),
             pltpu.SemaphoreType.DMA((ahead,)),
-            pltpu.SemaphoreType.DMA((chunks,)),
+            pltpu.SemaphoreType.DMA((chunks + 1,)),
             pltpu.SemaphoreType.DMA,
             pltpu.SemaphoreType.DMA,
             pltpu.SemaphoreType.DMA,
@@ -436,7 +452,7 @@
             pltpu.SemaphoreType.DMA((per_group,)),
         ],
         compiler_params=pltpu.CompilerParams(
-            collective_id=0, has_side_effects=True, vmem_limit_bytes=63 * 1024 * 1024
+            collective_id=0, has_side_effects=True, vmem_limit_bytes=67_043_328
         ),
         name="fused",
     )(partner, qtable, densities, amplitudes, grid_map, coulomb)

time: 767 us -> 766 us (level)
  no operation moved by 1% of the time
where the time goes in v5:
time: 766 us; the launch traced here: 764 us
  Pallas kernels  763 us (100%)
    pallas_call x1, Pallas kernels, fused(): pl.pallas_call(functools.partial(fused_kernel, kgrp, band), in_specs=[sca...  763 us

profile of v5, /device:TPU:0, one launch (start us, length us, event | category | flops | bytes accessed | tf_op | source)
XLA Modules:
  0.0 764.2 jit_solution(2166605447450987005)
XLA Ops:
  0.0 762.7 %fused.1 = (bf16[32,32,2,4,2,8,128]{6,5,4,3,2,1,0:T(8,128)(2,1)}, bf16[16,2,8,128]{3,2,1,0:T(8,128)(2,1)}) custom-call(s32[8]{0:T(128)} %partner_ref.1, s32[8]{0:T(128)} %qtable_ref.1, bf16[2,16,128,4096]{3,2,1,0:T(8,128)(2,1)} %densities_ref.1, bf16[2,8,128,128]{3,2,1,0:T(8,128)(2,1)} %amplitudes_ref.1, s32[64,4096]{1,0:T(8,128)} %grid_ref.1, ...), custom_call_target="tpu_custom_call" | custom-call | tf_op jit(solution)/shard_map/fused/pallas_call | solution.py:413
  762.7 1.5 copy.8
